TPU v7x, 32 devices: a whole 2x2x4 slice. The times are simulated.
32 devices in a mesh: block: 8 (over y, x, core), sub: 4 (over z).
Axes of the slice: x: 2, y: 2, z: 4, core: 2. Of those that a mesh axis runs over, the one named last changes fastest.
Arguments:
- source: float32 [8, 16, 128, 128], P('block', 'sub'), may hold values from -48 to 48
- trans_x: float32 [8, 16, 128, 128], P('block', 'sub'), may hold values from 0.1 to 10
- trans_y: float32 [8, 16, 128, 128], P('block', 'sub'), may hold values from 0.1 to 10
- trans_z: float32 [8, 16, 128, 128], P('block', 'sub'), may hold values from 0.1 to 10
- mortar_bot: float32 [8, 16, 128, 256], P('block', 'sub'), may hold values from -0.375 to 0.375
- mortar_top: float32 [8, 16, 128, 256], P('block', 'sub'), may hold values from -0.375 to 0.375
Outputs:
- pressure: float32 [8, 16, 128, 128], P('block', 'sub')
- mortar: float32 [8, 256], P('block', 'sub')
All inputs are finite; a program needn't handle non-finite values.
Results may differ from a plain program's by a relative error of at most 0.0003.
Values sent between devices are 32-bit elements; how exact they have to be, the bound alone decides.
No kernel may reach another device: no remote copies, remote signals or barrier semaphores. Data moves between devices by JAX's collectives and lax.ppermute only.
A program may use at most 64 MiB of HBM per device.

v0:
```python
import jax
import jax.numpy as jnp
from jax import lax
from jax.sharding import PartitionSpec as P

PASSES = 3
OUTER = 2
RELAX = 0.8
MORTAR_STEP = 0.05
HIGHEST = lax.Precision.HIGHEST


def from_behind(block, axis, distance):
    devices = range(lax.axis_size(axis))
    route = [(i - distance, i) for i in devices if i - distance in devices]
    return lax.ppermute(block, axis, route)


def with_halo(value, sides, width):
    for axis, dim in sides:
        devices, length = (lax.axis_size(axis), value.shape[dim])
        up = [(i, (i + 1) % devices) for i in range(devices - 1)]
        down = [(j, i) for i, j in up]
        last = lax.slice_in_dim(value, length - width, length, axis=dim)
        leading = lax.slice_in_dim(value, 0, width, axis=dim)
        before = lax.ppermute(last, axis, up)
        after = lax.ppermute(leading, axis, down)
        value = jnp.concatenate([before, value, after], axis=dim)
    return value


def below_of(values, axis):
    widths = [(0, 0)] * values.ndim
    widths[axis] = (1, 0)
    return lax.slice_in_dim(jnp.pad(values, widths), 0, values.shape[axis], axis=axis)


def above_of(values, axis):
    widths = [(0, 0)] * values.ndim
    widths[axis] = (0, 1)
    return lax.slice_in_dim(jnp.pad(values, widths), 1, values.shape[axis] + 1, axis=axis)


def widen_one(values):
    return jnp.pad(values, ((0, 0), (1, 1), (0, 0), (0, 0)))


def relax_pass(padded, rhs_part, offset, coeffs):
    coupling_x, coupling_next, coupling_y, coupling_z, diagonal = coeffs
    count = padded.shape[1] - 2

    def window(values):
        return values[:, offset : offset + count]

    centre = padded[:, 1:-1]
    part_x = window(coupling_x)
    part_next = window(coupling_next)
    part_y = window(coupling_y)
    part_z = window(coupling_z)
    part_diag = window(diagonal)
    applied = (
        part_diag * centre
        - part_x * padded[:, :-2]
        - part_next * padded[:, 2:]
        - part_y * below_of(centre, 2)
        - above_of(part_y, 2) * above_of(centre, 2)
        - part_z * below_of(centre, 3)
        - above_of(part_z, 3) * above_of(centre, 3)
    )
    return centre + RELAX * (rhs_part - applied) / part_diag


def shards(source, trans_x, trans_y, trans_z, mortar_bot, mortar_top):
    local_x = source.shape[1]
    rows_y = source.shape[2]
    cells_z = source.shape[3]
    mortars = mortar_bot.shape[3]
    sub_count = lax.axis_size("sub")
    block_count = lax.axis_size("block")
    sub_index = lax.axis_index("sub")
    block_index = lax.axis_index("block")
    share = mortars // sub_count
    depth = 1
    global_x = lax.broadcasted_iota(jnp.int32, source.shape, 1) + sub_index * local_x
    masked_x = jnp.where(global_x > 0, trans_x, 0.0)
    upper_layer = from_behind(masked_x[:, 0:1], "sub", -1)
    coupling_x = widen_one(masked_x)
    coupling_next = widen_one(jnp.concatenate([masked_x[:, 1:], upper_layer], axis=1))
    raw_y = widen_one(trans_y)
    raw_z = widen_one(trans_z)
    wide_shape = coupling_x.shape
    wide_x = lax.broadcasted_iota(jnp.int32, wide_shape, 1) - depth + sub_index * local_x
    index_y = lax.broadcasted_iota(jnp.int32, wide_shape, 2)
    index_z = lax.broadcasted_iota(jnp.int32, wide_shape, 3)
    coupling_y = jnp.where(index_y > 0, raw_y, 0.0)
    coupling_z = jnp.where(index_z > 0, raw_z, 0.0)
    dirichlet_bot = jnp.where((index_z == 0) & (block_index > 0), raw_z, 0.0)
    dirichlet_top = jnp.where(
        (index_z == cells_z - 1) & (block_index < block_count - 1), raw_z, 0.0
    )
    diagonal = (
        coupling_x
        + coupling_next
        + coupling_y
        + above_of(coupling_y, 2)
        + coupling_z
        + above_of(coupling_z, 3)
        + dirichlet_bot
        + dirichlet_top
    )
    inside = (wide_x >= 0) & (wide_x < local_x * sub_count)
    diagonal = jnp.where(inside, diagonal, 1.0)
    coeffs = (coupling_x, coupling_next, coupling_y, coupling_z, diagonal)
    local_bot = dirichlet_bot[:, depth : depth + local_x]
    local_top = dirichlet_top[:, depth : depth + local_x]
    face_bot = mortar_bot.reshape(local_x * rows_y, mortars)
    face_top = mortar_top.reshape(local_x * rows_y, mortars)
    pressure = jnp.zeros_like(source)
    mortar_pair = jnp.zeros((2, mortars), jnp.float32)
    final_row = jnp.zeros((share,), jnp.float32)
    for outer_round in range(OUTER):
        bottom_data = jnp.dot(face_bot, mortar_pair[0], precision=HIGHEST).reshape(
            1, local_x, rows_y
        )
        top_data = jnp.dot(face_top, mortar_pair[1], precision=HIGHEST).reshape(1, local_x, rows_y)
        rhs = source + local_bot * bottom_data[..., None] + local_top * top_data[..., None]
        for pass_round in range(PASSES):
            padded = with_halo(pressure, (("sub", 1),), 1)
            pressure = relax_pass(padded, rhs, 1, coeffs)
        flux_bot = local_bot[..., 0] * (pressure[..., 0] - bottom_data)
        flux_top = local_top[..., cells_z - 1] * (pressure[..., cells_z - 1] - top_data)
        terms = jnp.stack(
            [
                jnp.dot(flux_bot.reshape(-1), face_bot, precision=HIGHEST),
                jnp.dot(flux_top.reshape(-1), face_top, precision=HIGHEST),
            ]
        )
        shares = lax.psum(terms, "sub")
        current_pair = mortar_pair
        nearby = with_halo(shares[None], (("block", 0),), 1)
        jumps = jnp.stack([nearby[0, 1] + nearby[1, 0], nearby[1, 1] + nearby[2, 0]])
        updated = current_pair + MORTAR_STEP * jumps
        mortar_pair = updated
        final_row = lax.dynamic_slice_in_dim(updated[1], sub_index * share, share, 0)
    return (pressure, final_row[None])


def solution(mesh):
    return jax.shard_map(
        shards,
        mesh=mesh,
        in_specs=(
            P("block", "sub", None, None),
            P("block", "sub", None, None),
            P("block", "sub", None, None),
            P("block", "sub", None, None),
            P("block", "sub", None, None),
            P("block", "sub", None, None),
        ),
        out_specs=(P("block", "sub", None, None), P("block", "sub")),
        check_vma=False,
    )
```

profile of v0, /device:TPU:12, one launch (start us, length us, event | category | flops | bytes accessed | tf_op | source)
XLA Modules:
  0.0 99.8 jit_solution(6974258271982418281)
XLA Ops:
  0.7 2.5 %collective-permute-start.2 = (f32[1,1,128,128]{2,1,3,0:T(1,128)S(1)}, f32[1,1,128,128]{2,1,3,0:T(1,128)S(1)}, u32[]{:S(2)}, u32[]{:S(2)}) collective-permute-start(f32[1,1,128,128]{2,1,3,0:T(1,128)S(1)} %broadcast.138), channel_id=1, source_target_pairs={{1,0},{2,1},{3,2},{5,4},{6,5},{7,6},{9,8},{10,9},{11,10},{13,12},{... | collective-permute-start | bytes 196616 | tf_op jit(solution)/shard_map/ppermute | solution.py:27
  3.2 3.5 %collective-permute-start.1 = (f32[1,1,128,128]{2,1,3,0:T(1,128)S(1)}, f32[1,1,128,128]{2,1,3,0:T(1,128)S(1)}, u32[]{:S(2)}, u32[]{:S(2)}) collective-permute-start(f32[1,1,128,128]{2,1,3,0:T(1,128)S(1)} %broadcast.138), channel_id=1, source_target_pairs={{0,1},{1,2},{2,3},{4,5},{5,6},{6,7},{8,9},{9,10},{10,11},{12,13},{... | collective-permute-start | bytes 196616 | tf_op jit(solution)/shard_map/ppermute | solution.py:26
  6.7 1.1 %copy.10 = f32[1,4,128,128]{2,1,3,0:T(4,128)S(1)} copy(f32[1,4,128,128]{3,2,1,0:T(8,128)} %param.7) | data formatting | bytes 524288 | tf_op args[1]
  7.8 0.1 broadcast_select_fusion
  8.0 2.4 %collective-permute-start = (f32[1,1,128,128]{2,1,3,0:T(1,128)S(1)}, f32[1,1,128,128]{2,1,3,0:T(1,128)S(1)}, u32[]{:S(2)}, u32[]{:S(2)}) collective-permute-start(f32[1,1,128,128]{2,1,3,0:T(1,128)S(1)} %slice.352), channel_id=1, source_target_pairs={{1,0},{2,1},{3,2},{5,4},{6,5},{7,6},{9,8},{10,9},{11,10},{13,12},{... | collective-permute-start | bytes 196616 | tf_op jit(solution)/shard_map/ppermute | solution.py:16
  10.4 0.1 slice.351
  10.5 0.1 slice.359
  10.5 0.5 fusion.116
  11.1 0.5 fusion.118
  11.6 0.4 copy-done.6
  12.1 0.1 copy.9
  12.2 0.8 copy-done.7
  13.0 0.1 copy.11
  13.2 0.8 copy-done.8
  14.0 0.1 copy.8
  14.2 0.1 pad_maximum_fusion.10
  14.3 0.8 pad_select_fusion.2
  15.1 0.1 slice.355
  15.3 0.2 pad_slice_fusion
  15.6 1.0 %fusion.9 = (f32[1,4,128,128]{2,1,3,0:T(4,128)S(1)}, f32[1,4,128,128]{2,1,3,0:T(4,128)S(1)}, f32[1,4,128,128]{2,1,3,0:T(4,128)S(1)}) fusion(f32[1,4,128,128]{2,1,3,0:T(4,128)S(1)} %slice.355, f32[1,4,128,128]{2,1,3,0:T(4,128)S(1)} %broadcast_in_dim.23, f32[1,1,128,128]{2,1,3,0:T(1,128)S(1)} %collective-permute-done.1, ...), kind=kLoop, calls=%fused_computation.48 | loop fusion | flops 1835008 | bytes 4329480 | tf_op jit(solution)/shard_map/div | solution.py:70
  16.6 0.1 fusion.128
  16.7 3.5 %collective-permute-start.3 = (f32[1,1,128,128]{2,1,3,0:T(1,128)S(1)}, f32[1,1,128,128]{2,1,3,0:T(1,128)S(1)}, u32[]{:S(2)}, u32[]{:S(2)}) collective-permute-start(f32[1,1,128,128]{2,1,3,0:T(1,128)S(1)} %get-tuple-element.23), channel_id=1, source_target_pairs={{0,1},{1,2},{2,3},{4,5},{5,6},{6,7},{8,9},{9,10},{10,11},{12,13},{... | collective-permute-start | bytes 196616 | tf_op jit(solution)/shard_map/ppermute | solution.py:26
  20.2 2.4 %collective-permute-start.4 = (f32[1,1,128,128]{2,1,3,0:T(1,128)S(1)}, f32[1,1,128,128]{2,1,3,0:T(1,128)S(1)}, u32[]{:S(2)}, u32[]{:S(2)}) collective-permute-start(f32[1,1,128,128]{2,1,3,0:T(1,128)S(1)} %get-tuple-element.24), channel_id=1, source_target_pairs={{1,0},{2,1},{3,2},{5,4},{6,5},{7,6},{9,8},{10,9},{11,10},{13,12},{... | collective-permute-start | bytes 196616 | tf_op jit(solution)/shard_map/ppermute | solution.py:27
  22.6 0.3 collective-permute-done.3
  22.9 3.5 %collective-permute-done.4 = f32[1,1,128,128]{2,1,3,0:T(1,128)S(1)} collective-permute-done((f32[1,1,128,128]{2,1,3,0:T(1,128)S(1)}, f32[1,1,128,128]{2,1,3,0:T(1,128)S(1)}, u32[]{:S(2)}, u32[]{:S(2)}) %collective-permute-start.4) | collective-permute-done | bytes 65568 | tf_op jit(solution)/shard_map/ppermute | solution.py:27
  26.4 0.8 fusion.96
  27.2 0.1 fusion.127
  27.3 3.5 %collective-permute-start.5 = (f32[1,1,128,128]{2,1,3,0:T(1,128)S(1)}, f32[1,1,128,128]{2,1,3,0:T(1,128)S(1)}, u32[]{:S(2)}, u32[]{:S(2)}) collective-permute-start(f32[1,1,128,128]{2,1,3,0:T(1,128)S(1)} %get-tuple-element.21), channel_id=1, source_target_pairs={{0,1},{1,2},{2,3},{4,5},{5,6},{6,7},{8,9},{9,10},{10,11},{12,13},{... | collective-permute-start | bytes 196616 | tf_op jit(solution)/shard_map/ppermute | solution.py:26
  30.8 2.4 %collective-permute-start.6 = (f32[1,1,128,128]{2,1,3,0:T(1,128)S(1)}, f32[1,1,128,128]{2,1,3,0:T(1,128)S(1)}, u32[]{:S(2)}, u32[]{:S(2)}) collective-permute-start(f32[1,1,128,128]{2,1,3,0:T(1,128)S(1)} %get-tuple-element.22), channel_id=1, source_target_pairs={{1,0},{2,1},{3,2},{5,4},{6,5},{7,6},{9,8},{10,9},{11,10},{13,12},{... | collective-permute-start | bytes 196616 | tf_op jit(solution)/shard_map/ppermute | solution.py:27
  33.2 0.3 collective-permute-done.5
  33.5 3.5 %collective-permute-done.6 = f32[1,1,128,128]{2,1,3,0:T(1,128)S(1)} collective-permute-done((f32[1,1,128,128]{2,1,3,0:T(1,128)S(1)}, f32[1,1,128,128]{2,1,3,0:T(1,128)S(1)}, u32[]{:S(2)}, u32[]{:S(2)}) %collective-permute-start.6) | collective-permute-done | bytes 65568 | tf_op jit(solution)/shard_map/ppermute | solution.py:27
  36.9 0.8 fusion.91
  37.8 0.3 convolution_bitcast_fusion.3
  38.1 0.3 convolution_bitcast_fusion.2
  38.5 8.8 %psum.14 = f32[1,2,256]{2,1,0:T(2,128)S(1)} all-reduce(f32[1,2,256]{2,1,0:T(2,128)S(1)} %maximum_bitcast_fusion), channel_id=1, replica_groups=mesh['block'=8,'sub'=4] {'sub'}, use_global_device_ids=true, to_apply=%region_0.1 | all-reduce | flops 512 | bytes 4096 | tf_op jit(solution)/shard_map/psum | solution.py:138
  47.3 1.9 %collective-permute-start.8 = (f32[1,2,256]{2,1,0:T(2,128)S(1)}, f32[1,2,256]{2,1,0:T(2,128)S(1)}, u32[]{:S(2)}, u32[]{:S(2)}) collective-permute-start(f32[1,2,256]{2,1,0:T(2,128)S(1)} %psum.14), channel_id=1, source_target_pairs={{4,0},{8,4},{12,8},{16,12},{20,16},{24,20},{28,24},{5,1},{9,5},{13... | collective-permute-start | bytes 6152 | tf_op jit(solution)/shard_map/ppermute | solution.py:27
  49.2 2.4 %collective-permute-start.7 = (f32[1,2,256]{2,1,0:T(2,128)S(1)}, f32[1,2,256]{2,1,0:T(2,128)S(1)}, u32[]{:S(2)}, u32[]{:S(2)}) collective-permute-start(f32[1,2,256]{2,1,0:T(2,128)S(1)} %psum.14), channel_id=1, source_target_pairs={{0,4},{4,8},{8,12},{12,16},{16,20},{20,24},{24,28},{1,5},{5,9},{9,... | collective-permute-start | bytes 6152 | tf_op jit(solution)/shard_map/ppermute | solution.py:26
  51.6 0.1 fusion.126
  51.7 1.9 %collective-permute-start.9 = (f32[1,1,128,128]{2,1,3,0:T(1,128)S(1)}, f32[1,1,128,128]{2,1,3,0:T(1,128)S(1)}, u32[]{:S(2)}, u32[]{:S(2)}) collective-permute-start(f32[1,1,128,128]{2,1,3,0:T(1,128)S(1)} %get-tuple-element.19), channel_id=1, source_target_pairs={{0,1},{1,2},{2,3},{4,5},{5,6},{6,7},{8,9},{9,10},{10,11},{12,13},{... | collective-permute-start | bytes 196616 | tf_op jit(solution)/shard_map/ppermute | solution.py:26
  53.6 3.9 %collective-permute-start.10 = (f32[1,1,128,128]{2,1,3,0:T(1,128)S(1)}, f32[1,1,128,128]{2,1,3,0:T(1,128)S(1)}, u32[]{:S(2)}, u32[]{:S(2)}) collective-permute-start(f32[1,1,128,128]{2,1,3,0:T(1,128)S(1)} %get-tuple-element.20), channel_id=1, source_target_pairs={{1,0},{2,1},{3,2},{5,4},{6,5},{7,6},{9,8},{10,9},{11,10},{13,12},{... | collective-permute-start | bytes 196616 | tf_op jit(solution)/shard_map/ppermute | solution.py:27
  57.6 0.5 fusion.112
  58.1 0.5 fusion.109
  58.7 1.7 %collective-permute-done.10 = f32[1,1,128,128]{2,1,3,0:T(1,128)S(1)} collective-permute-done((f32[1,1,128,128]{2,1,3,0:T(1,128)S(1)}, f32[1,1,128,128]{2,1,3,0:T(1,128)S(1)}, u32[]{:S(2)}, u32[]{:S(2)}) %collective-permute-start.10) | collective-permute-done | bytes 65568 | tf_op jit(solution)/shard_map/ppermute | solution.py:27
  60.4 0.9 fusion.86
  61.3 0.1 fusion.125
  61.4 3.1 %collective-permute-start.11 = (f32[1,1,128,128]{2,1,3,0:T(1,128)S(1)}, f32[1,1,128,128]{2,1,3,0:T(1,128)S(1)}, u32[]{:S(2)}, u32[]{:S(2)}) collective-permute-start(f32[1,1,128,128]{2,1,3,0:T(1,128)S(1)} %get-tuple-element.15), channel_id=1, source_target_pairs={{0,1},{1,2},{2,3},{4,5},{5,6},{6,7},{8,9},{9,10},{10,11},{12,13},{... | collective-permute-start | bytes 196616 | tf_op jit(solution)/shard_map/ppermute | solution.py:26
  64.5 2.8 %collective-permute-start.12 = (f32[1,1,128,128]{2,1,3,0:T(1,128)S(1)}, f32[1,1,128,128]{2,1,3,0:T(1,128)S(1)}, u32[]{:S(2)}, u32[]{:S(2)}) collective-permute-start(f32[1,1,128,128]{2,1,3,0:T(1,128)S(1)} %get-tuple-element.16), channel_id=1, source_target_pairs={{1,0},{2,1},{3,2},{5,4},{6,5},{7,6},{9,8},{10,9},{11,10},{13,12},{... | collective-permute-start | bytes 196616 | tf_op jit(solution)/shard_map/ppermute | solution.py:27
  67.3 0.3 collective-permute-done.11
  67.6 3.1 %collective-permute-done.12 = f32[1,1,128,128]{2,1,3,0:T(1,128)S(1)} collective-permute-done((f32[1,1,128,128]{2,1,3,0:T(1,128)S(1)}, f32[1,1,128,128]{2,1,3,0:T(1,128)S(1)}, u32[]{:S(2)}, u32[]{:S(2)}) %collective-permute-start.12) | collective-permute-done | bytes 65568 | tf_op jit(solution)/shard_map/ppermute | solution.py:27
  70.6 0.8 fusion.81
  71.4 0.1 fusion.124
  71.6 1.9 %collective-permute-start.13 = (f32[1,1,128,128]{2,1,3,0:T(1,128)S(1)}, f32[1,1,128,128]{2,1,3,0:T(1,128)S(1)}, u32[]{:S(2)}, u32[]{:S(2)}) collective-permute-start(f32[1,1,128,128]{2,1,3,0:T(1,128)S(1)} %get-tuple-element.13), channel_id=1, source_target_pairs={{0,1},{1,2},{2,3},{4,5},{5,6},{6,7},{8,9},{9,10},{10,11},{12,13},{... | collective-permute-start | bytes 196616 | tf_op jit(solution)/shard_map/ppermute | solution.py:26
  73.5 3.9 %collective-permute-start.14 = (f32[1,1,128,128]{2,1,3,0:T(1,128)S(1)}, f32[1,1,128,128]{2,1,3,0:T(1,128)S(1)}, u32[]{:S(2)}, u32[]{:S(2)}) collective-permute-start(f32[1,1,128,128]{2,1,3,0:T(1,128)S(1)} %get-tuple-element.14), channel_id=1, source_target_pairs={{1,0},{2,1},{3,2},{5,4},{6,5},{7,6},{9,8},{10,9},{11,10},{13,12},{... | collective-permute-start | bytes 196616 | tf_op jit(solution)/shard_map/ppermute | solution.py:27
  77.4 0.3 collective-permute-done.13
  77.7 1.9 %collective-permute-done.14 = f32[1,1,128,128]{2,1,3,0:T(1,128)S(1)} collective-permute-done((f32[1,1,128,128]{2,1,3,0:T(1,128)S(1)}, f32[1,1,128,128]{2,1,3,0:T(1,128)S(1)}, u32[]{:S(2)}, u32[]{:S(2)}) %collective-permute-start.14) | collective-permute-done | bytes 65568 | tf_op jit(solution)/shard_map/ppermute | solution.py:27
  79.6 0.8 fusion.76
  80.5 0.3 convolution_bitcast_fusion.1
  80.7 0.3 convolution_bitcast_fusion
  81.1 10.3 %psum.15 = f32[1,2,256]{2,1,0:T(2,128)S(1)} all-reduce(f32[1,2,256]{2,1,0:T(2,128)S(1)} %maximum_bitcast_fusion.1), channel_id=1, replica_groups=mesh['block'=8,'sub'=4] {'sub'}, use_global_device_ids=true, to_apply=%region_1.2 | all-reduce | flops 512 | bytes 4096 | tf_op jit(solution)/shard_map/psum | solution.py:138
  91.5 1.9 %collective-permute-start.16 = (f32[1,2,256]{2,1,0:T(2,128)S(1)}, f32[1,2,256]{2,1,0:T(2,128)S(1)}, u32[]{:S(2)}, u32[]{:S(2)}) collective-permute-start(f32[1,2,256]{2,1,0:T(2,128)S(1)} %psum.15), channel_id=1, source_target_pairs={{4,0},{8,4},{12,8},{16,12},{20,16},{24,20},{28,24},{5,1},{9,5},{13... | collective-permute-start | bytes 6152 | tf_op jit(solution)/shard_map/ppermute | solution.py:27
  93.4 2.4 %collective-permute-start.15 = (f32[1,2,256]{2,1,0:T(2,128)S(1)}, f32[1,2,256]{2,1,0:T(2,128)S(1)}, u32[]{:S(2)}, u32[]{:S(2)}) collective-permute-start(f32[1,2,256]{2,1,0:T(2,128)S(1)} %psum.15), channel_id=1, source_target_pairs={{0,4},{4,8},{8,12},{12,16},{16,20},{20,24},{24,28},{1,5},{5,9},{9,... | collective-permute-start | bytes 6152 | tf_op jit(solution)/shard_map/ppermute | solution.py:26
  95.8 0.8 copy.13
  96.7 2.5 %collective-permute-done.15 = f32[1,2,256]{2,1,0:T(2,128)S(1)} collective-permute-done((f32[1,2,256]{2,1,0:T(2,128)S(1)}, f32[1,2,256]{2,1,0:T(2,128)S(1)}, u32[]{:S(2)}, u32[]{:S(2)}) %collective-permute-start.15) | collective-permute-done | bytes 2080 | tf_op jit(solution)/shard_map/ppermute | solution.py:26
  99.2 0.6 fusion.114
  (39 shorter events, 0.5 us)
Async XLA Ops:
  0.6 10.5 %copy-start = (f32[1,4,128,256]{3,2,1,0:T(8,128)S(1)}, f32[1,4,128,256]{3,2,1,0:T(8,128)}, u32[]{:S(2)}) copy-start(f32[1,4,128,256]{3,2,1,0:T(8,128)} %param.10) | copy-start | bytes 1572868
  0.7 14.8 %collective-permute-start.2 = (f32[1,1,128,128]{2,1,3,0:T(1,128)S(1)}, f32[1,1,128,128]{2,1,3,0:T(1,128)S(1)}, u32[]{:S(2)}, u32[]{:S(2)}) collective-permute-start(f32[1,1,128,128]{2,1,3,0:T(1,128)S(1)} %broadcast.138), channel_id=1, source_target_pairs={{1,0},{2,1},{3,2},{5,4},{6,5},{7,6},{9,8},{10,9},{11,10},{13,12},{... | collective-permute-start | bytes 196616 | tf_op jit(solution)/shard_map/ppermute | solution.py:27
  3.2 12.4 %collective-permute-start.1 = (f32[1,1,128,128]{2,1,3,0:T(1,128)S(1)}, f32[1,1,128,128]{2,1,3,0:T(1,128)S(1)}, u32[]{:S(2)}, u32[]{:S(2)}) collective-permute-start(f32[1,1,128,128]{2,1,3,0:T(1,128)S(1)} %broadcast.138), channel_id=1, source_target_pairs={{0,1},{1,2},{2,3},{4,5},{5,6},{6,7},{8,9},{9,10},{10,11},{12,13},{... | collective-permute-start | bytes 196616 | tf_op jit(solution)/shard_map/ppermute | solution.py:26
  7.8 2.7 %copy-start.1 = (f32[1,4,128,256]{3,2,1,0:T(8,128)S(1)}, f32[1,4,128,256]{3,2,1,0:T(8,128)}, u32[]{:S(2)}) copy-start(f32[1,4,128,256]{3,2,1,0:T(8,128)} %param.11) | copy-start | bytes 1572868
  8.0 6.2 %collective-permute-start = (f32[1,1,128,128]{2,1,3,0:T(1,128)S(1)}, f32[1,1,128,128]{2,1,3,0:T(1,128)S(1)}, u32[]{:S(2)}, u32[]{:S(2)}) collective-permute-start(f32[1,1,128,128]{2,1,3,0:T(1,128)S(1)} %slice.352), channel_id=1, source_target_pairs={{1,0},{2,1},{3,2},{5,4},{6,5},{7,6},{9,8},{10,9},{11,10},{13,12},{... | collective-permute-start | bytes 196616 | tf_op jit(solution)/shard_map/ppermute | solution.py:16
  11.1 1.0 copy-start.6
  12.0 0.9 copy-start.7
  13.0 0.9 copy-start.8
  15.1 22.7 %copy-start.2 = (f32[1,6,128,128]{2,1,3,0:T(8,128)}, f32[1,6,128,128]{2,1,3,0:T(8,128)S(1)}, u32[]{:S(2)}) copy-start(f32[1,6,128,128]{2,1,3,0:T(8,128)S(1)} %get-tuple-element.25) | copy-start | bytes 1179652
  15.1 22.7 %copy-start.4 = (f32[1,6,128,128]{2,1,3,0:T(8,128)}, f32[1,6,128,128]{2,1,3,0:T(8,128)S(1)}, u32[]{:S(2)}) copy-start(f32[1,6,128,128]{2,1,3,0:T(8,128)S(1)} %get-tuple-element.26) | copy-start | bytes 1179652
  16.7 6.2 %collective-permute-start.3 = (f32[1,1,128,128]{2,1,3,0:T(1,128)S(1)}, f32[1,1,128,128]{2,1,3,0:T(1,128)S(1)}, u32[]{:S(2)}, u32[]{:S(2)}) collective-permute-start(f32[1,1,128,128]{2,1,3,0:T(1,128)S(1)} %get-tuple-element.23), channel_id=1, source_target_pairs={{0,1},{1,2},{2,3},{4,5},{5,6},{6,7},{8,9},{9,10},{10,11},{12,13},{... | collective-permute-start | bytes 196616 | tf_op jit(solution)/shard_map/ppermute | solution.py:26
  20.2 6.2 %collective-permute-start.4 = (f32[1,1,128,128]{2,1,3,0:T(1,128)S(1)}, f32[1,1,128,128]{2,1,3,0:T(1,128)S(1)}, u32[]{:S(2)}, u32[]{:S(2)}) collective-permute-start(f32[1,1,128,128]{2,1,3,0:T(1,128)S(1)} %get-tuple-element.24), channel_id=1, source_target_pairs={{1,0},{2,1},{3,2},{5,4},{6,5},{7,6},{9,8},{10,9},{11,10},{13,12},{... | collective-permute-start | bytes 196616 | tf_op jit(solution)/shard_map/ppermute | solution.py:27
  27.3 6.2 %collective-permute-start.5 = (f32[1,1,128,128]{2,1,3,0:T(1,128)S(1)}, f32[1,1,128,128]{2,1,3,0:T(1,128)S(1)}, u32[]{:S(2)}, u32[]{:S(2)}) collective-permute-start(f32[1,1,128,128]{2,1,3,0:T(1,128)S(1)} %get-tuple-element.21), channel_id=1, source_target_pairs={{0,1},{1,2},{2,3},{4,5},{5,6},{6,7},{8,9},{9,10},{10,11},{12,13},{... | collective-permute-start | bytes 196616 | tf_op jit(solution)/shard_map/ppermute | solution.py:26
  30.8 6.2 %collective-permute-start.6 = (f32[1,1,128,128]{2,1,3,0:T(1,128)S(1)}, f32[1,1,128,128]{2,1,3,0:T(1,128)S(1)}, u32[]{:S(2)}, u32[]{:S(2)}) collective-permute-start(f32[1,1,128,128]{2,1,3,0:T(1,128)S(1)} %get-tuple-element.22), channel_id=1, source_target_pairs={{1,0},{2,1},{3,2},{5,4},{6,5},{7,6},{9,8},{10,9},{11,10},{13,12},{... | collective-permute-start | bytes 196616 | tf_op jit(solution)/shard_map/ppermute | solution.py:27
  47.3 10.3 %collective-permute-start.8 = (f32[1,2,256]{2,1,0:T(2,128)S(1)}, f32[1,2,256]{2,1,0:T(2,128)S(1)}, u32[]{:S(2)}, u32[]{:S(2)}) collective-permute-start(f32[1,2,256]{2,1,0:T(2,128)S(1)} %psum.14), channel_id=1, source_target_pairs={{4,0},{8,4},{12,8},{16,12},{20,16},{24,20},{28,24},{5,1},{9,5},{13... | collective-permute-start | bytes 6152 | tf_op jit(solution)/shard_map/ppermute | solution.py:27
  49.2 8.4 %collective-permute-start.7 = (f32[1,2,256]{2,1,0:T(2,128)S(1)}, f32[1,2,256]{2,1,0:T(2,128)S(1)}, u32[]{:S(2)}, u32[]{:S(2)}) collective-permute-start(f32[1,2,256]{2,1,0:T(2,128)S(1)} %psum.14), channel_id=1, source_target_pairs={{0,4},{4,8},{8,12},{12,16},{16,20},{20,24},{24,28},{1,5},{5,9},{9,... | collective-permute-start | bytes 6152 | tf_op jit(solution)/shard_map/ppermute | solution.py:26
  51.7 7.0 %collective-permute-start.9 = (f32[1,1,128,128]{2,1,3,0:T(1,128)S(1)}, f32[1,1,128,128]{2,1,3,0:T(1,128)S(1)}, u32[]{:S(2)}, u32[]{:S(2)}) collective-permute-start(f32[1,1,128,128]{2,1,3,0:T(1,128)S(1)} %get-tuple-element.19), channel_id=1, source_target_pairs={{0,1},{1,2},{2,3},{4,5},{5,6},{6,7},{8,9},{9,10},{10,11},{12,13},{... | collective-permute-start | bytes 196616 | tf_op jit(solution)/shard_map/ppermute | solution.py:26
  53.6 6.7 %collective-permute-start.10 = (f32[1,1,128,128]{2,1,3,0:T(1,128)S(1)}, f32[1,1,128,128]{2,1,3,0:T(1,128)S(1)}, u32[]{:S(2)}, u32[]{:S(2)}) collective-permute-start(f32[1,1,128,128]{2,1,3,0:T(1,128)S(1)} %get-tuple-element.20), channel_id=1, source_target_pairs={{1,0},{2,1},{3,2},{5,4},{6,5},{7,6},{9,8},{10,9},{11,10},{13,12},{... | collective-permute-start | bytes 196616 | tf_op jit(solution)/shard_map/ppermute | solution.py:27
  57.6 2.7 %copy-start.3 = (f32[1,6,128,128]{2,1,3,0:T(8,128)S(1)}, f32[1,6,128,128]{2,1,3,0:T(8,128)}, u32[]{:S(2)}) copy-start(f32[1,6,128,128]{2,1,3,0:T(8,128)} %copy-done.2) | copy-start | bytes 1179652
  57.6 2.7 %copy-start.5 = (f32[1,6,128,128]{2,1,3,0:T(8,128)S(1)}, f32[1,6,128,128]{2,1,3,0:T(8,128)}, u32[]{:S(2)}) copy-start(f32[1,6,128,128]{2,1,3,0:T(8,128)} %copy-done.4) | copy-start | bytes 1179652
  61.4 6.2 %collective-permute-start.11 = (f32[1,1,128,128]{2,1,3,0:T(1,128)S(1)}, f32[1,1,128,128]{2,1,3,0:T(1,128)S(1)}, u32[]{:S(2)}, u32[]{:S(2)}) collective-permute-start(f32[1,1,128,128]{2,1,3,0:T(1,128)S(1)} %get-tuple-element.15), channel_id=1, source_target_pairs={{0,1},{1,2},{2,3},{4,5},{5,6},{6,7},{8,9},{9,10},{10,11},{12,13},{... | collective-permute-start | bytes 196616 | tf_op jit(solution)/shard_map/ppermute | solution.py:26
  64.5 6.2 %collective-permute-start.12 = (f32[1,1,128,128]{2,1,3,0:T(1,128)S(1)}, f32[1,1,128,128]{2,1,3,0:T(1,128)S(1)}, u32[]{:S(2)}, u32[]{:S(2)}) collective-permute-start(f32[1,1,128,128]{2,1,3,0:T(1,128)S(1)} %get-tuple-element.16), channel_id=1, source_target_pairs={{1,0},{2,1},{3,2},{5,4},{6,5},{7,6},{9,8},{10,9},{11,10},{13,12},{... | collective-permute-start | bytes 196616 | tf_op jit(solution)/shard_map/ppermute | solution.py:27
  71.6 6.2 %collective-permute-start.13 = (f32[1,1,128,128]{2,1,3,0:T(1,128)S(1)}, f32[1,1,128,128]{2,1,3,0:T(1,128)S(1)}, u32[]{:S(2)}, u32[]{:S(2)}) collective-permute-start(f32[1,1,128,128]{2,1,3,0:T(1,128)S(1)} %get-tuple-element.13), channel_id=1, source_target_pairs={{0,1},{1,2},{2,3},{4,5},{5,6},{6,7},{8,9},{9,10},{10,11},{12,13},{... | collective-permute-start | bytes 196616 | tf_op jit(solution)/shard_map/ppermute | solution.py:26
  73.5 6.2 %collective-permute-start.14 = (f32[1,1,128,128]{2,1,3,0:T(1,128)S(1)}, f32[1,1,128,128]{2,1,3,0:T(1,128)S(1)}, u32[]{:S(2)}, u32[]{:S(2)}) collective-permute-start(f32[1,1,128,128]{2,1,3,0:T(1,128)S(1)} %get-tuple-element.14), channel_id=1, source_target_pairs={{1,0},{2,1},{3,2},{5,4},{6,5},{7,6},{9,8},{10,9},{11,10},{13,12},{... | collective-permute-start | bytes 196616 | tf_op jit(solution)/shard_map/ppermute | solution.py:27
  91.5 5.2 %collective-permute-start.16 = (f32[1,2,256]{2,1,0:T(2,128)S(1)}, f32[1,2,256]{2,1,0:T(2,128)S(1)}, u32[]{:S(2)}, u32[]{:S(2)}) collective-permute-start(f32[1,2,256]{2,1,0:T(2,128)S(1)} %psum.15), channel_id=1, source_target_pairs={{4,0},{8,4},{12,8},{16,12},{20,16},{24,20},{28,24},{5,1},{9,5},{13... | collective-permute-start | bytes 6152 | tf_op jit(solution)/shard_map/ppermute | solution.py:27
  93.4 5.8 %collective-permute-start.15 = (f32[1,2,256]{2,1,0:T(2,128)S(1)}, f32[1,2,256]{2,1,0:T(2,128)S(1)}, u32[]{:S(2)}, u32[]{:S(2)}) collective-permute-start(f32[1,2,256]{2,1,0:T(2,128)S(1)} %psum.15), channel_id=1, source_target_pairs={{0,4},{4,8},{8,12},{12,16},{16,20},{20,24},{24,28},{1,5},{5,9},{9,... | collective-permute-start | bytes 6152 | tf_op jit(solution)/shard_map/ppermute | solution.py:26
where the time goes:
time: 100 us; the launch traced here: 99.8 us
  starting transfers between devices  46.2 us (46%)
  blocking collectives  19.1 us (19%)
  waiting for transfers between devices  17.4 us (17%)
  other arithmetic  7.05 us (7%)
  local copies, waits for them, and re-layouts  5.58 us (6%)
  matrix products  3.32 us (3%)
  between operations  1.12 us (1%)
    ppermute x8, starting transfers between devices, with_halo(): before = lax.ppermute(last, axis, up)  22.2 us
    ppermute x8, starting transfers between devices, with_halo(): after = lax.ppermute(leading, axis, down)  21.7 us
    psum x2, blocking collectives, shards(): shares = lax.psum(terms, 'sub')  19.1 us
    ppermute x8, waiting for transfers between devices, with_halo(): after = lax.ppermute(leading, axis, down)  13.7 us
    unnamed x23, local copies, waits for them, and re-layouts  4.42 us
    add x5, other arithmetic, relax_pass(): return centre + RELAX * (rhs_part - applied) / part_diag  4.21 us
    ppermute x8, waiting for transfers between devices, with_halo(): before = lax.ppermute(last, axis, up)  3.74 us
    ppermute x1, starting transfers between devices, from_behind(): return lax.ppermute(block, axis, route)  2.36 us
  transfers between devices with their start and end apart: 17, of which 10 were waited for; matrix products, arithmetic and copies ran while one was open for 6% of the time, Pallas kernels for 0%

commit v1 on v0

--- a/solution.py
+++ b/solution.py
@@ -135,7 +135,8 @@
                 jnp.dot(flux_top.reshape(-1), face_top, precision=HIGHEST),
             ]
         )
-        shares = lax.psum(terms, "sub")
+        terms_2 = lax.all_gather(terms, "sub")
+        shares = jnp.sum(terms_2, axis=0)
         current_pair = mortar_pair
         nearby = with_halo(shares[None], (("block", 0),), 1)
         jumps = jnp.stack([nearby[0, 1] + nearby[1, 0], nearby[1, 1] + nearby[2, 0]])

time: 100 us -> 106 us (1.060)
  the two profiles are of different devices: /device:TPU:12 before, /device:TPU:4 now
where the time goes in v1:
time: 106 us; the launch traced here: 105 us
  starting transfers between devices  36.9 us (35%)
  waiting for transfers between devices  27.4 us (26%)
  blocking collectives  23.9 us (23%)
  other arithmetic  7.08 us (7%)
  local copies, waits for them, and re-layouts  5.58 us (5%)
  matrix products  3.32 us (3%)
  between operations  1.12 us (1%)
    all_gather x2, blocking collectives, shards(): terms_2 = lax.all_gather(terms, 'sub')  23.9 us
    ppermute x8, starting transfers between devices, with_halo(): before = lax.ppermute(last, axis, up)  23.9 us
    ppermute x8, waiting for transfers between devices, with_halo(): after = lax.ppermute(leading, axis, down)  21.4 us
    ppermute x8, starting transfers between devices, with_halo(): after = lax.ppermute(leading, axis, down)  11.7 us
    ppermute x8, waiting for transfers between devices, with_halo(): before = lax.ppermute(last, axis, up)  4.87 us
    unnamed x23, local copies, waits for them, and re-layouts  4.42 us
    add x5, other arithmetic, relax_pass(): return centre + RELAX * (rhs_part - applied) / part_diag  4.2 us
  transfers between devices with their start and end apart: 17, of which 11 were waited for; matrix products, arithmetic and copies ran while one was open for 6% of the time, Pallas kernels for 0%

profile of v1, /device:TPU:4, one launch (start us, length us, event | category | flops | bytes accessed | tf_op | source)
XLA Modules:
  0.0 105.2 jit_solution(12419961814943340151)
XLA Ops:
  0.7 1.4 %collective-permute-start.2 = (f32[1,1,128,128]{2,1,3,0:T(1,128)S(1)}, f32[1,1,128,128]{2,1,3,0:T(1,128)S(1)}, u32[]{:S(2)}, u32[]{:S(2)}) collective-permute-start(f32[1,1,128,128]{2,1,3,0:T(1,128)S(1)} %broadcast.138), channel_id=1, source_target_pairs={{1,0},{2,1},{3,2},{5,4},{6,5},{7,6},{9,8},{10,9},{11,10},{13,12},{... | collective-permute-start | bytes 196616 | tf_op jit(solution)/shard_map/ppermute | solution.py:27
  2.1 4.5 %collective-permute-start.1 = (f32[1,1,128,128]{2,1,3,0:T(1,128)S(1)}, f32[1,1,128,128]{2,1,3,0:T(1,128)S(1)}, u32[]{:S(2)}, u32[]{:S(2)}) collective-permute-start(f32[1,1,128,128]{2,1,3,0:T(1,128)S(1)} %broadcast.138), channel_id=1, source_target_pairs={{0,1},{1,2},{2,3},{4,5},{5,6},{6,7},{8,9},{9,10},{10,11},{12,13},{... | collective-permute-start | bytes 196616 | tf_op jit(solution)/shard_map/ppermute | solution.py:26
  6.7 1.1 %copy.16 = f32[1,4,128,128]{2,1,3,0:T(4,128)S(1)} copy(f32[1,4,128,128]{3,2,1,0:T(8,128)} %param.7) | data formatting | bytes 524288 | tf_op args[1]
  7.8 0.1 broadcast_select_fusion
  8.0 1.3 %collective-permute-start = (f32[1,1,128,128]{2,1,3,0:T(1,128)S(1)}, f32[1,1,128,128]{2,1,3,0:T(1,128)S(1)}, u32[]{:S(2)}, u32[]{:S(2)}) collective-permute-start(f32[1,1,128,128]{2,1,3,0:T(1,128)S(1)} %slice.352), channel_id=1, source_target_pairs={{1,0},{2,1},{3,2},{5,4},{6,5},{7,6},{9,8},{10,9},{11,10},{13,12},{... | collective-permute-start | bytes 196616 | tf_op jit(solution)/shard_map/ppermute | solution.py:16
  9.4 0.1 slice.359
  9.5 0.5 fusion.116
  10.0 0.5 fusion.118
  10.6 0.4 copy-done.6
  11.0 0.1 copy.15
  11.1 0.8 copy-done.7
  11.9 0.1 copy.17
  12.1 0.8 copy-done.8
  12.9 0.1 copy.14
  13.1 1.1 %collective-permute-done = f32[1,1,128,128]{2,1,3,0:T(1,128)S(1)} collective-permute-done((f32[1,1,128,128]{2,1,3,0:T(1,128)S(1)}, f32[1,1,128,128]{2,1,3,0:T(1,128)S(1)}, u32[]{:S(2)}, u32[]{:S(2)}) %collective-permute-start) | collective-permute-done | bytes 65568 | tf_op jit(solution)/shard_map/ppermute | solution.py:16
  14.2 0.1 pad_maximum_fusion.10
  14.3 0.8 pad_select_fusion.2
  15.1 0.1 slice.355
  15.3 0.2 pad_slice_fusion
  15.6 1.0 fusion.9
  16.6 0.1 fusion.128
  16.7 3.5 %collective-permute-start.3 = (f32[1,1,128,128]{2,1,3,0:T(1,128)S(1)}, f32[1,1,128,128]{2,1,3,0:T(1,128)S(1)}, u32[]{:S(2)}, u32[]{:S(2)}) collective-permute-start(f32[1,1,128,128]{2,1,3,0:T(1,128)S(1)} %get-tuple-element.25), channel_id=1, source_target_pairs={{0,1},{1,2},{2,3},{4,5},{5,6},{6,7},{8,9},{9,10},{10,11},{12,13},{... | collective-permute-start | bytes 196616 | tf_op jit(solution)/shard_map/ppermute | solution.py:26
  20.2 1.3 %collective-permute-start.4 = (f32[1,1,128,128]{2,1,3,0:T(1,128)S(1)}, f32[1,1,128,128]{2,1,3,0:T(1,128)S(1)}, u32[]{:S(2)}, u32[]{:S(2)}) collective-permute-start(f32[1,1,128,128]{2,1,3,0:T(1,128)S(1)} %get-tuple-element.26), channel_id=1, source_target_pairs={{1,0},{2,1},{3,2},{5,4},{6,5},{7,6},{9,8},{10,9},{11,10},{13,12},{... | collective-permute-start | bytes 196616 | tf_op jit(solution)/shard_map/ppermute | solution.py:27
  21.5 0.6 collective-permute-done.3
  22.1 4.3 %collective-permute-done.4 = f32[1,1,128,128]{2,1,3,0:T(1,128)S(1)} collective-permute-done((f32[1,1,128,128]{2,1,3,0:T(1,128)S(1)}, f32[1,1,128,128]{2,1,3,0:T(1,128)S(1)}, u32[]{:S(2)}, u32[]{:S(2)}) %collective-permute-start.4) | collective-permute-done | bytes 65568 | tf_op jit(solution)/shard_map/ppermute | solution.py:27
  26.4 0.8 fusion.96
  27.2 0.1 fusion.127
  27.3 3.5 %collective-permute-start.5 = (f32[1,1,128,128]{2,1,3,0:T(1,128)S(1)}, f32[1,1,128,128]{2,1,3,0:T(1,128)S(1)}, u32[]{:S(2)}, u32[]{:S(2)}) collective-permute-start(f32[1,1,128,128]{2,1,3,0:T(1,128)S(1)} %get-tuple-element.23), channel_id=1, source_target_pairs={{0,1},{1,2},{2,3},{4,5},{5,6},{6,7},{8,9},{9,10},{10,11},{12,13},{... | collective-permute-start | bytes 196616 | tf_op jit(solution)/shard_map/ppermute | solution.py:26
  30.8 1.3 %collective-permute-start.6 = (f32[1,1,128,128]{2,1,3,0:T(1,128)S(1)}, f32[1,1,128,128]{2,1,3,0:T(1,128)S(1)}, u32[]{:S(2)}, u32[]{:S(2)}) collective-permute-start(f32[1,1,128,128]{2,1,3,0:T(1,128)S(1)} %get-tuple-element.24), channel_id=1, source_target_pairs={{1,0},{2,1},{3,2},{5,4},{6,5},{7,6},{9,8},{10,9},{11,10},{13,12},{... | collective-permute-start | bytes 196616 | tf_op jit(solution)/shard_map/ppermute | solution.py:27
  32.1 0.6 collective-permute-done.5
  32.7 4.3 %collective-permute-done.6 = f32[1,1,128,128]{2,1,3,0:T(1,128)S(1)} collective-permute-done((f32[1,1,128,128]{2,1,3,0:T(1,128)S(1)}, f32[1,1,128,128]{2,1,3,0:T(1,128)S(1)}, u32[]{:S(2)}, u32[]{:S(2)}) %collective-permute-start.6) | collective-permute-done | bytes 65568 | tf_op jit(solution)/shard_map/ppermute | solution.py:27
  37.0 0.8 fusion.91
  37.8 0.3 convolution_bitcast_fusion.3
  38.1 0.3 convolution_bitcast_fusion.2
  38.5 11.9 %all-gather.2 = f32[4,2,256]{2,1,0:T(2,128)S(1)} all-gather(f32[1,2,256]{2,1,0:T(2,128)S(1)} %maximum_bitcast_fusion), channel_id=2, replica_groups=mesh['block'=8,'sub'=4] {'sub'}, dimensions={0}, use_global_device_ids=true | all-gather | bytes 10240 | tf_op jit(solution)/shard_map/all_gather | solution.py:138
  50.4 1.9 %collective-permute-start.8 = (f32[1,2,256]{2,1,0:T(2,128)S(1)}, f32[1,2,256]{2,1,0:T(2,128)S(1)}, u32[]{:S(2)}, u32[]{:S(2)}) collective-permute-start(f32[1,2,256]{2,1,0:T(2,128)S(1)} %bitcast.117), channel_id=1, source_target_pairs={{4,0},{8,4},{12,8},{16,12},{20,16},{24,20},{28,24},{5,1},{9,5},{13... | collective-permute-start | bytes 6152 | tf_op jit(solution)/shard_map/ppermute | solution.py:27
  52.4 2.4 %collective-permute-start.7 = (f32[1,2,256]{2,1,0:T(2,128)S(1)}, f32[1,2,256]{2,1,0:T(2,128)S(1)}, u32[]{:S(2)}, u32[]{:S(2)}) collective-permute-start(f32[1,2,256]{2,1,0:T(2,128)S(1)} %bitcast.118), channel_id=1, source_target_pairs={{0,4},{4,8},{8,12},{12,16},{16,20},{20,24},{24,28},{1,5},{5,9},{9,... | collective-permute-start | bytes 6152 | tf_op jit(solution)/shard_map/ppermute | solution.py:26
  54.8 0.1 fusion.126
  54.9 2.0 %collective-permute-start.9 = (f32[1,1,128,128]{2,1,3,0:T(1,128)S(1)}, f32[1,1,128,128]{2,1,3,0:T(1,128)S(1)}, u32[]{:S(2)}, u32[]{:S(2)}) collective-permute-start(f32[1,1,128,128]{2,1,3,0:T(1,128)S(1)} %get-tuple-element.21), channel_id=1, source_target_pairs={{0,1},{1,2},{2,3},{4,5},{5,6},{6,7},{8,9},{9,10},{10,11},{12,13},{... | collective-permute-start | bytes 196616 | tf_op jit(solution)/shard_map/ppermute | solution.py:26
  56.9 1.3 %collective-permute-start.10 = (f32[1,1,128,128]{2,1,3,0:T(1,128)S(1)}, f32[1,1,128,128]{2,1,3,0:T(1,128)S(1)}, u32[]{:S(2)}, u32[]{:S(2)}) collective-permute-start(f32[1,1,128,128]{2,1,3,0:T(1,128)S(1)} %get-tuple-element.22), channel_id=1, source_target_pairs={{1,0},{2,1},{3,2},{5,4},{6,5},{7,6},{9,8},{10,9},{11,10},{13,12},{... | collective-permute-start | bytes 196616 | tf_op jit(solution)/shard_map/ppermute | solution.py:27
  58.3 0.5 fusion.112
  58.8 0.5 fusion.109
  59.4 4.3 %collective-permute-done.10 = f32[1,1,128,128]{2,1,3,0:T(1,128)S(1)} collective-permute-done((f32[1,1,128,128]{2,1,3,0:T(1,128)S(1)}, f32[1,1,128,128]{2,1,3,0:T(1,128)S(1)}, u32[]{:S(2)}, u32[]{:S(2)}) %collective-permute-start.10) | collective-permute-done | bytes 65568 | tf_op jit(solution)/shard_map/ppermute | solution.py:27
  63.7 0.9 fusion.86
  64.6 0.1 fusion.125
  64.7 3.3 %collective-permute-start.11 = (f32[1,1,128,128]{2,1,3,0:T(1,128)S(1)}, f32[1,1,128,128]{2,1,3,0:T(1,128)S(1)}, u32[]{:S(2)}, u32[]{:S(2)}) collective-permute-start(f32[1,1,128,128]{2,1,3,0:T(1,128)S(1)} %get-tuple-element.17), channel_id=1, source_target_pairs={{0,1},{1,2},{2,3},{4,5},{5,6},{6,7},{8,9},{9,10},{10,11},{12,13},{... | collective-permute-start | bytes 196616 | tf_op jit(solution)/shard_map/ppermute | solution.py:26
  68.0 1.3 %collective-permute-start.12 = (f32[1,1,128,128]{2,1,3,0:T(1,128)S(1)}, f32[1,1,128,128]{2,1,3,0:T(1,128)S(1)}, u32[]{:S(2)}, u32[]{:S(2)}) collective-permute-start(f32[1,1,128,128]{2,1,3,0:T(1,128)S(1)} %get-tuple-element.18), channel_id=1, source_target_pairs={{1,0},{2,1},{3,2},{5,4},{6,5},{7,6},{9,8},{10,9},{11,10},{13,12},{... | collective-permute-start | bytes 196616 | tf_op jit(solution)/shard_map/ppermute | solution.py:27
  69.3 0.6 collective-permute-done.11
  69.9 4.3 %collective-permute-done.12 = f32[1,1,128,128]{2,1,3,0:T(1,128)S(1)} collective-permute-done((f32[1,1,128,128]{2,1,3,0:T(1,128)S(1)}, f32[1,1,128,128]{2,1,3,0:T(1,128)S(1)}, u32[]{:S(2)}, u32[]{:S(2)}) %collective-permute-start.12) | collective-permute-done | bytes 65568 | tf_op jit(solution)/shard_map/ppermute | solution.py:27
  74.2 0.8 fusion.81
  75.0 0.1 fusion.124
  75.1 2.2 %collective-permute-start.13 = (f32[1,1,128,128]{2,1,3,0:T(1,128)S(1)}, f32[1,1,128,128]{2,1,3,0:T(1,128)S(1)}, u32[]{:S(2)}, u32[]{:S(2)}) collective-permute-start(f32[1,1,128,128]{2,1,3,0:T(1,128)S(1)} %get-tuple-element.15), channel_id=1, source_target_pairs={{0,1},{1,2},{2,3},{4,5},{5,6},{6,7},{8,9},{9,10},{10,11},{12,13},{... | collective-permute-start | bytes 196616 | tf_op jit(solution)/shard_map/ppermute | solution.py:26
  77.3 1.3 %collective-permute-start.14 = (f32[1,1,128,128]{2,1,3,0:T(1,128)S(1)}, f32[1,1,128,128]{2,1,3,0:T(1,128)S(1)}, u32[]{:S(2)}, u32[]{:S(2)}) collective-permute-start(f32[1,1,128,128]{2,1,3,0:T(1,128)S(1)} %get-tuple-element.16), channel_id=1, source_target_pairs={{1,0},{2,1},{3,2},{5,4},{6,5},{7,6},{9,8},{10,9},{11,10},{13,12},{... | collective-permute-start | bytes 196616 | tf_op jit(solution)/shard_map/ppermute | solution.py:27
  78.6 0.6 collective-permute-done.13
  79.2 4.3 %collective-permute-done.14 = f32[1,1,128,128]{2,1,3,0:T(1,128)S(1)} collective-permute-done((f32[1,1,128,128]{2,1,3,0:T(1,128)S(1)}, f32[1,1,128,128]{2,1,3,0:T(1,128)S(1)}, u32[]{:S(2)}, u32[]{:S(2)}) %collective-permute-start.14) | collective-permute-done | bytes 65568 | tf_op jit(solution)/shard_map/ppermute | solution.py:27
  83.5 0.8 fusion.76
  84.3 0.3 convolution_bitcast_fusion.1
  84.6 0.3 convolution_bitcast_fusion
  85.0 11.9 %all-gather.3 = f32[4,2,256]{2,1,0:T(2,128)S(1)} all-gather(f32[1,2,256]{2,1,0:T(2,128)S(1)} %maximum_bitcast_fusion.1), channel_id=3, replica_groups=mesh['block'=8,'sub'=4] {'sub'}, dimensions={0}, use_global_device_ids=true | all-gather | bytes 10240 | tf_op jit(solution)/shard_map/all_gather | solution.py:138
  96.9 1.9 %collective-permute-start.16 = (f32[1,2,256]{2,1,0:T(2,128)S(1)}, f32[1,2,256]{2,1,0:T(2,128)S(1)}, u32[]{:S(2)}, u32[]{:S(2)}) collective-permute-start(f32[1,2,256]{2,1,0:T(2,128)S(1)} %bitcast.114), channel_id=1, source_target_pairs={{4,0},{8,4},{12,8},{16,12},{20,16},{24,20},{28,24},{5,1},{9,5},{13... | collective-permute-start | bytes 6152 | tf_op jit(solution)/shard_map/ppermute | solution.py:27
  98.8 2.4 %collective-permute-start.15 = (f32[1,2,256]{2,1,0:T(2,128)S(1)}, f32[1,2,256]{2,1,0:T(2,128)S(1)}, u32[]{:S(2)}, u32[]{:S(2)}) collective-permute-start(f32[1,2,256]{2,1,0:T(2,128)S(1)} %bitcast.115), channel_id=1, source_target_pairs={{0,4},{4,8},{8,12},{12,16},{16,20},{20,24},{24,28},{1,5},{5,9},{9,... | collective-permute-start | bytes 6152 | tf_op jit(solution)/shard_map/ppermute | solution.py:26
  101.3 0.8 copy.19
  102.1 2.5 %collective-permute-done.15 = f32[1,2,256]{2,1,0:T(2,128)S(1)} collective-permute-done((f32[1,2,256]{2,1,0:T(2,128)S(1)}, f32[1,2,256]{2,1,0:T(2,128)S(1)}, u32[]{:S(2)}, u32[]{:S(2)}) %collective-permute-start.15) | collective-permute-done | bytes 2080 | tf_op jit(solution)/shard_map/ppermute | solution.py:26
  104.6 0.6 fusion.114
  (41 shorter events, 0.6 us)
Async XLA Ops:
  0.6 9.4 %copy-start = (f32[1,4,128,256]{3,2,1,0:T(8,128)S(1)}, f32[1,4,128,256]{3,2,1,0:T(8,128)}, u32[]{:S(2)}) copy-start(f32[1,4,128,256]{3,2,1,0:T(8,128)} %param.10) | copy-start | bytes 1572868
  0.7 14.8 %collective-permute-start.2 = (f32[1,1,128,128]{2,1,3,0:T(1,128)S(1)}, f32[1,1,128,128]{2,1,3,0:T(1,128)S(1)}, u32[]{:S(2)}, u32[]{:S(2)}) collective-permute-start(f32[1,1,128,128]{2,1,3,0:T(1,128)S(1)} %broadcast.138), channel_id=1, source_target_pairs={{1,0},{2,1},{3,2},{5,4},{6,5},{7,6},{9,8},{10,9},{11,10},{13,12},{... | collective-permute-start | bytes 196616 | tf_op jit(solution)/shard_map/ppermute | solution.py:27
  2.1 13.4 %collective-permute-start.1 = (f32[1,1,128,128]{2,1,3,0:T(1,128)S(1)}, f32[1,1,128,128]{2,1,3,0:T(1,128)S(1)}, u32[]{:S(2)}, u32[]{:S(2)}) collective-permute-start(f32[1,1,128,128]{2,1,3,0:T(1,128)S(1)} %broadcast.138), channel_id=1, source_target_pairs={{0,1},{1,2},{2,3},{4,5},{5,6},{6,7},{8,9},{9,10},{10,11},{12,13},{... | collective-permute-start | bytes 196616 | tf_op jit(solution)/shard_map/ppermute | solution.py:26
  7.8 1.7 %copy-start.1 = (f32[1,4,128,256]{3,2,1,0:T(8,128)S(1)}, f32[1,4,128,256]{3,2,1,0:T(8,128)}, u32[]{:S(2)}) copy-start(f32[1,4,128,256]{3,2,1,0:T(8,128)} %param.11) | copy-start | bytes 1572868
  8.0 6.2 %collective-permute-start = (f32[1,1,128,128]{2,1,3,0:T(1,128)S(1)}, f32[1,1,128,128]{2,1,3,0:T(1,128)S(1)}, u32[]{:S(2)}, u32[]{:S(2)}) collective-permute-start(f32[1,1,128,128]{2,1,3,0:T(1,128)S(1)} %slice.352), channel_id=1, source_target_pairs={{1,0},{2,1},{3,2},{5,4},{6,5},{7,6},{9,8},{10,9},{11,10},{13,12},{... | collective-permute-start | bytes 196616 | tf_op jit(solution)/shard_map/ppermute | solution.py:16
  10.0 1.0 copy-start.6
  11.0 0.9 copy-start.7
  11.9 0.9 copy-start.8
  15.1 22.7 %copy-start.2 = (f32[1,6,128,128]{2,1,3,0:T(8,128)}, f32[1,6,128,128]{2,1,3,0:T(8,128)S(1)}, u32[]{:S(2)}) copy-start(f32[1,6,128,128]{2,1,3,0:T(8,128)S(1)} %get-tuple-element.27) | copy-start | bytes 1179652
  15.1 22.7 %copy-start.4 = (f32[1,6,128,128]{2,1,3,0:T(8,128)}, f32[1,6,128,128]{2,1,3,0:T(8,128)S(1)}, u32[]{:S(2)}) copy-start(f32[1,6,128,128]{2,1,3,0:T(8,128)S(1)} %get-tuple-element.28) | copy-start | bytes 1179652
  16.7 5.4 %collective-permute-start.3 = (f32[1,1,128,128]{2,1,3,0:T(1,128)S(1)}, f32[1,1,128,128]{2,1,3,0:T(1,128)S(1)}, u32[]{:S(2)}, u32[]{:S(2)}) collective-permute-start(f32[1,1,128,128]{2,1,3,0:T(1,128)S(1)} %get-tuple-element.25), channel_id=1, source_target_pairs={{0,1},{1,2},{2,3},{4,5},{5,6},{6,7},{8,9},{9,10},{10,11},{12,13},{... | collective-permute-start | bytes 196616 | tf_op jit(solution)/shard_map/ppermute | solution.py:26
  20.2 6.2 %collective-permute-start.4 = (f32[1,1,128,128]{2,1,3,0:T(1,128)S(1)}, f32[1,1,128,128]{2,1,3,0:T(1,128)S(1)}, u32[]{:S(2)}, u32[]{:S(2)}) collective-permute-start(f32[1,1,128,128]{2,1,3,0:T(1,128)S(1)} %get-tuple-element.26), channel_id=1, source_target_pairs={{1,0},{2,1},{3,2},{5,4},{6,5},{7,6},{9,8},{10,9},{11,10},{13,12},{... | collective-permute-start | bytes 196616 | tf_op jit(solution)/shard_map/ppermute | solution.py:27
  27.3 5.4 %collective-permute-start.5 = (f32[1,1,128,128]{2,1,3,0:T(1,128)S(1)}, f32[1,1,128,128]{2,1,3,0:T(1,128)S(1)}, u32[]{:S(2)}, u32[]{:S(2)}) collective-permute-start(f32[1,1,128,128]{2,1,3,0:T(1,128)S(1)} %get-tuple-element.23), channel_id=1, source_target_pairs={{0,1},{1,2},{2,3},{4,5},{5,6},{6,7},{8,9},{9,10},{10,11},{12,13},{... | collective-permute-start | bytes 196616 | tf_op jit(solution)/shard_map/ppermute | solution.py:26
  30.8 6.2 %collective-permute-start.6 = (f32[1,1,128,128]{2,1,3,0:T(1,128)S(1)}, f32[1,1,128,128]{2,1,3,0:T(1,128)S(1)}, u32[]{:S(2)}, u32[]{:S(2)}) collective-permute-start(f32[1,1,128,128]{2,1,3,0:T(1,128)S(1)} %get-tuple-element.24), channel_id=1, source_target_pairs={{1,0},{2,1},{3,2},{5,4},{6,5},{7,6},{9,8},{10,9},{11,10},{13,12},{... | collective-permute-start | bytes 196616 | tf_op jit(solution)/shard_map/ppermute | solution.py:27
  50.4 7.8 %collective-permute-start.8 = (f32[1,2,256]{2,1,0:T(2,128)S(1)}, f32[1,2,256]{2,1,0:T(2,128)S(1)}, u32[]{:S(2)}, u32[]{:S(2)}) collective-permute-start(f32[1,2,256]{2,1,0:T(2,128)S(1)} %bitcast.117), channel_id=1, source_target_pairs={{4,0},{8,4},{12,8},{16,12},{20,16},{24,20},{28,24},{5,1},{9,5},{13... | collective-permute-start | bytes 6152 | tf_op jit(solution)/shard_map/ppermute | solution.py:27
  52.4 5.9 %collective-permute-start.7 = (f32[1,2,256]{2,1,0:T(2,128)S(1)}, f32[1,2,256]{2,1,0:T(2,128)S(1)}, u32[]{:S(2)}, u32[]{:S(2)}) collective-permute-start(f32[1,2,256]{2,1,0:T(2,128)S(1)} %bitcast.118), channel_id=1, source_target_pairs={{0,4},{4,8},{8,12},{12,16},{16,20},{20,24},{24,28},{1,5},{5,9},{9,... | collective-permute-start | bytes 6152 | tf_op jit(solution)/shard_map/ppermute | solution.py:26
  54.9 4.5 %collective-permute-start.9 = (f32[1,1,128,128]{2,1,3,0:T(1,128)S(1)}, f32[1,1,128,128]{2,1,3,0:T(1,128)S(1)}, u32[]{:S(2)}, u32[]{:S(2)}) collective-permute-start(f32[1,1,128,128]{2,1,3,0:T(1,128)S(1)} %get-tuple-element.21), channel_id=1, source_target_pairs={{0,1},{1,2},{2,3},{4,5},{5,6},{6,7},{8,9},{9,10},{10,11},{12,13},{... | collective-permute-start | bytes 196616 | tf_op jit(solution)/shard_map/ppermute | solution.py:26
  56.9 6.7 %collective-permute-start.10 = (f32[1,1,128,128]{2,1,3,0:T(1,128)S(1)}, f32[1,1,128,128]{2,1,3,0:T(1,128)S(1)}, u32[]{:S(2)}, u32[]{:S(2)}) collective-permute-start(f32[1,1,128,128]{2,1,3,0:T(1,128)S(1)} %get-tuple-element.22), channel_id=1, source_target_pairs={{1,0},{2,1},{3,2},{5,4},{6,5},{7,6},{9,8},{10,9},{11,10},{13,12},{... | collective-permute-start | bytes 196616 | tf_op jit(solution)/shard_map/ppermute | solution.py:27
  58.3 5.4 %copy-start.3 = (f32[1,6,128,128]{2,1,3,0:T(8,128)S(1)}, f32[1,6,128,128]{2,1,3,0:T(8,128)}, u32[]{:S(2)}) copy-start(f32[1,6,128,128]{2,1,3,0:T(8,128)} %copy-done.2) | copy-start | bytes 1179652
  58.3 5.4 %copy-start.5 = (f32[1,6,128,128]{2,1,3,0:T(8,128)S(1)}, f32[1,6,128,128]{2,1,3,0:T(8,128)}, u32[]{:S(2)}) copy-start(f32[1,6,128,128]{2,1,3,0:T(8,128)} %copy-done.4) | copy-start | bytes 1179652
  64.7 5.2 %collective-permute-start.11 = (f32[1,1,128,128]{2,1,3,0:T(1,128)S(1)}, f32[1,1,128,128]{2,1,3,0:T(1,128)S(1)}, u32[]{:S(2)}, u32[]{:S(2)}) collective-permute-start(f32[1,1,128,128]{2,1,3,0:T(1,128)S(1)} %get-tuple-element.17), channel_id=1, source_target_pairs={{0,1},{1,2},{2,3},{4,5},{5,6},{6,7},{8,9},{9,10},{10,11},{12,13},{... | collective-permute-start | bytes 196616 | tf_op jit(solution)/shard_map/ppermute | solution.py:26
  68.0 6.2 %collective-permute-start.12 = (f32[1,1,128,128]{2,1,3,0:T(1,128)S(1)}, f32[1,1,128,128]{2,1,3,0:T(1,128)S(1)}, u32[]{:S(2)}, u32[]{:S(2)}) collective-permute-start(f32[1,1,128,128]{2,1,3,0:T(1,128)S(1)} %get-tuple-element.18), channel_id=1, source_target_pairs={{1,0},{2,1},{3,2},{5,4},{6,5},{7,6},{9,8},{10,9},{11,10},{13,12},{... | collective-permute-start | bytes 196616 | tf_op jit(solution)/shard_map/ppermute | solution.py:27
  75.1 4.1 %collective-permute-start.13 = (f32[1,1,128,128]{2,1,3,0:T(1,128)S(1)}, f32[1,1,128,128]{2,1,3,0:T(1,128)S(1)}, u32[]{:S(2)}, u32[]{:S(2)}) collective-permute-start(f32[1,1,128,128]{2,1,3,0:T(1,128)S(1)} %get-tuple-element.15), channel_id=1, source_target_pairs={{0,1},{1,2},{2,3},{4,5},{5,6},{6,7},{8,9},{9,10},{10,11},{12,13},{... | collective-permute-start | bytes 196616 | tf_op jit(solution)/shard_map/ppermute | solution.py:26
  77.3 6.2 %collective-permute-start.14 = (f32[1,1,128,128]{2,1,3,0:T(1,128)S(1)}, f32[1,1,128,128]{2,1,3,0:T(1,128)S(1)}, u32[]{:S(2)}, u32[]{:S(2)}) collective-permute-start(f32[1,1,128,128]{2,1,3,0:T(1,128)S(1)} %get-tuple-element.16), channel_id=1, source_target_pairs={{1,0},{2,1},{3,2},{5,4},{6,5},{7,6},{9,8},{10,9},{11,10},{13,12},{... | collective-permute-start | bytes 196616 | tf_op jit(solution)/shard_map/ppermute | solution.py:27
  96.9 5.2 %collective-permute-start.16 = (f32[1,2,256]{2,1,0:T(2,128)S(1)}, f32[1,2,256]{2,1,0:T(2,128)S(1)}, u32[]{:S(2)}, u32[]{:S(2)}) collective-permute-start(f32[1,2,256]{2,1,0:T(2,128)S(1)} %bitcast.114), channel_id=1, source_target_pairs={{4,0},{8,4},{12,8},{16,12},{20,16},{24,20},{28,24},{5,1},{9,5},{13... | collective-permute-start | bytes 6152 | tf_op jit(solution)/shard_map/ppermute | solution.py:27
  98.8 5.8 %collective-permute-start.15 = (f32[1,2,256]{2,1,0:T(2,128)S(1)}, f32[1,2,256]{2,1,0:T(2,128)S(1)}, u32[]{:S(2)}, u32[]{:S(2)}) collective-permute-start(f32[1,2,256]{2,1,0:T(2,128)S(1)} %bitcast.115), channel_id=1, source_target_pairs={{0,4},{4,8},{8,12},{12,16},{16,20},{20,24},{24,28},{1,5},{5,9},{9,... | collective-permute-start | bytes 6152 | tf_op jit(solution)/shard_map/ppermute | solution.py:26
